TPU v7x, 128 devices: a whole 4x4x4 slice. The times are simulated.
128 devices in a mesh: row: 8 (over y, core), col: 16 (over x, z).
Axes of the slice: x: 4, y: 4, z: 4, core: 2. Of those that a mesh axis runs over, the one named last changes fastest.
Arguments:
- contribution: float32 [8, 8, 4, 16, 128, 128], P(None, 'row', None, 'col'), may hold values from -6 to 6
- parent_tiles: float32 [16, 8, 8, 16, 128, 128], P(None, 'row', None, 'col'), may hold values from -6 to 6
- row_basis: float32 [8, 8, 64, 128], P(None, 'row'), may hold values from -2.4 to 2.4
- pivot_basis: float32 [8, 8, 64, 2048], P(None, 'row', None, 'col'), may hold values from -0.125 to 0.125
- tile_ranks: int32 [64], replicated, may hold values from 16 to 64, as said below
- block_map: int32 [64], replicated, may hold values from 0 to 127, as said below
- panel_start: int32 [1], replicated, may hold values from 0 to 63
- pivot_inverse: float32 [512, 512], replicated
Outputs:
- updated_parent: float32 [16, 8, 8, 16, 128, 128], P(None, 'row', None, 'col')
Inputs may be any that keep to these rules, and one draw needn't show every extreme that they name: `tile_ranks`: multiples of 16; both 16 and 64 occur. `block_map`: child tile row u * 16 + l, for 0 <= l < 16, maps to parent tile row 2 * 16 * u + h_u + l with 0 <= h_u < 16; the 4 values h_u are distinct modulo 8.
All inputs are finite; a program needn't handle non-finite values.
Results may differ from a plain program's by a relative error of at most 0.0003.
Values sent between devices are 32-bit elements; how exact they have to be, the bound alone decides.
No kernel may reach another device: no remote copies, remote signals or barrier semaphores. Data moves between devices by JAX's collectives and lax.ppermute only.
A program may use at most 128 MiB of HBM per device.

v0:
```python
import jax
import jax.numpy as jnp
from jax import lax
from jax.sharding import PartitionSpec as P

PANEL_T = 4
highest = lax.Precision.HIGHEST


def spread_2(x, axis, root):
    mine = lax.axis_index(axis) == root
    return lax.psum(jnp.where(mine, x, jnp.zeros_like(x)), axis)


def from_behind(x, axis, by):
    count = lax.axis_size(axis)
    return lax.ppermute(x, axis, [(i, (i + by) % count) for i in range(count)])


def select_entries(lookup, wanted):
    matches = wanted[:, None] == jnp.arange(lookup.shape[0], dtype=jnp.int32)[None, :]
    return jnp.sum(jnp.where(matches, lookup[None, :], 0), axis=1)


def keep_ranks(factor, tile_index, rank_table):
    limits = select_entries(rank_table, tile_index)
    kept_cols = (jnp.arange(factor.shape[1], dtype=jnp.int32)[None, :] < limits[:, None]).astype(
        jnp.float32
    )
    return factor * kept_cols[:, :, None]


def every_other(stacked, groups, offset):
    shaped = stacked.reshape((groups, stacked.shape[0] // groups) + stacked.shape[1:])
    return lax.dynamic_index_in_dim(shaped, offset, axis=1, keepdims=False)


def per_device(
    contribution,
    parent_tiles,
    row_basis,
    pivot_basis,
    tile_ranks,
    block_map,
    panel_start,
    pivot_inverse,
):
    rows_grid = lax.axis_size("row")
    cols_grid = lax.axis_size("col")
    my_row = lax.axis_index("row")
    my_col = lax.axis_index("col")
    local_rows = contribution.shape[0]
    local_cols = contribution.shape[2]
    parent_rows = parent_tiles.shape[0]
    parent_cols = parent_tiles.shape[2]
    rank_max = row_basis.shape[2]
    per_block = cols_grid // rows_grid
    row_index = jnp.arange(local_rows, dtype=jnp.int32) * rows_grid + my_row
    col_index = jnp.arange(local_cols, dtype=jnp.int32) * cols_grid + my_col
    root_row = my_col % rows_grid
    offset = my_col // rows_grid
    own_basis = keep_ranks(row_basis[:, 0], row_index, tile_ranks)
    own_pivots = pivot_basis[:, 0]
    basis_picked = every_other(row_basis[:, 0], local_cols, offset)
    col_basis = spread_2(basis_picked, "row", root_row)
    all_pivots = lax.all_gather(pivot_basis, "row", axis=1, tiled=True)
    pivot_width = pivot_basis.shape[3]
    grouped = all_pivots.reshape(local_cols, cols_grid, rank_max, pivot_width)
    products = jnp.einsum(
        "trp,scup->cstru",
        own_pivots,
        grouped,
        precision=highest,
        preferred_element_type=jnp.float32,
    )
    weights = lax.psum_scatter(
        products.reshape(lax.axis_size("col") * local_cols, local_rows, rank_max * rank_max),
        "col",
        scatter_dimension=0,
        tiled=True,
    )
    weights = weights.reshape(local_cols, local_rows, rank_max, rank_max)
    col_basis = keep_ranks(col_basis, col_index, tile_ranks)
    half_product = jnp.einsum(
        "trx,stru->tsux", own_basis, weights, precision=highest, preferred_element_type=jnp.float32
    )
    update = jnp.einsum(
        "tsux,suy->tsxy",
        half_product,
        col_basis,
        precision=highest,
        preferred_element_type=jnp.float32,
    )
    lower_mask = (row_index[:, None] >= col_index[None, :])[:, :, None, None]
    payload = jnp.where(lower_mask, contribution[:, 0, :, 0] - update, jnp.float32(0.0))
    block_first = jnp.arange(local_cols, dtype=jnp.int32) * cols_grid
    shifts = select_entries(block_map, block_first) - 2 * block_first
    row_shift = jnp.repeat(shifts, per_block) % rows_grid
    for bit_index in range((rows_grid - 1).bit_length()):
        arrived = from_behind(payload, "row", 1 << bit_index)
        taken = row_shift // (1 << bit_index) % 2 == 1
        payload = jnp.where(taken[:, None, None, None], arrived, payload)
    for bit_index in range((cols_grid - 1).bit_length()):
        arrived = from_behind(payload, "col", 1 << bit_index)
        taken = shifts // (1 << bit_index) % 2 == 1
        payload = jnp.where(taken[None, :, None, None], arrived, payload)
    row_source = (my_row - row_shift) % rows_grid
    target_rows = (
        select_entries(block_map, jnp.arange(local_rows, dtype=jnp.int32) * rows_grid + row_source)
        // rows_grid
    )
    col_source = (my_col - shifts) % cols_grid
    target_cols = (
        select_entries(block_map, jnp.arange(local_cols, dtype=jnp.int32) * cols_grid + col_source)
        // cols_grid
    )
    row_place = (jnp.arange(parent_rows, dtype=jnp.int32)[:, None] == target_rows[None, :]).astype(
        jnp.float32
    )
    col_place = (jnp.arange(parent_cols, dtype=jnp.int32)[:, None] == target_cols[None, :]).astype(
        jnp.float32
    )
    spread = jnp.einsum(
        "at,tsxy->asxy", row_place, payload, precision=highest, preferred_element_type=jnp.float32
    )
    spread = jnp.einsum(
        "bs,asxy->abxy", col_place, spread, precision=highest, preferred_element_type=jnp.float32
    )
    assembled = parent_tiles[:, 0, :, 0] + spread
    start_col = panel_start[0]
    panel_parts = []
    for panel_index in range(PANEL_T):
        column_id = start_col + panel_index
        column = lax.dynamic_index_in_dim(assembled, column_id // cols_grid, axis=1, keepdims=False)
        panel_parts.append(spread_2(column, "col", column_id % cols_grid))
    row_panel = jnp.concatenate(panel_parts, axis=2)
    col_panel = spread_2(every_other(row_panel, parent_cols, offset), "row", root_row)
    scaled = jnp.einsum(
        "axp,pq->axq",
        row_panel,
        pivot_inverse,
        precision=highest,
        preferred_element_type=jnp.float32,
    )
    trailing = jnp.einsum(
        "axq,byq->abxy", scaled, col_panel, precision=highest, preferred_element_type=jnp.float32
    )
    big_rows = jnp.arange(parent_rows, dtype=jnp.int32) * rows_grid + my_row
    big_cols = jnp.arange(parent_cols, dtype=jnp.int32) * cols_grid + my_col
    window = (big_rows[:, None] >= big_cols[None, :]) & (big_cols[None, :] >= start_col + PANEL_T)
    result = jnp.where(window[:, :, None, None], assembled - trailing, assembled)
    return result[:, None, :, None]


def solution(mesh):
    placed = (
        P(None, "row", None, "col", None, None),
        P(None, "row", None, "col", None, None),
        P(None, "row", None, None),
        P(None, "row", None, "col"),
        P(),
        P(),
        P(),
        P(),
    )
    return jax.shard_map(
        per_device,
        mesh=mesh,
        in_specs=placed,
        out_specs=P(None, "row", None, "col", None, None),
        check_vma=False,
    )
```

profile of v0, /device:TPU:0, one launch (start us, length us, event | category | flops | bytes accessed | tf_op | source)
XLA Modules:
  0.0 810.4 jit_solution(2350074608308215927)
XLA Ops:
  6.5 0.7 all-gather.2.cloned.1.call-update
  7.3 29.4 %all-gather.2.cloned.1.call-done = f32[8,8,64,128]{3,2,1,0:T(8,128)} async-done(((f32[8,1,64,128]{3,2,1,0:T(8,128)}), f32[8,8,64,128]{3,2,1,0:T(8,128)}) %all-gather.2.cloned.1.call-update) | async-done | bytes 2097168 | tf_op jit(solution)/shard_map/all_gather | solution.py:66
  36.7 17.0 %convolution_bitcast_fusion = f32[16,4,8,64,64]{3,4,2,0,1:T(8,128)} fusion(f32[4,16,64,128,1]{3,2,4,1,0:T(8,128)} %bitcast.109, f32[8,1,64,128]{3,2,1,0:T(8,128)} %param.11), kind=kOutput, calls=%fused_computation.1 | convolution fusion | flops 3221225472 | bytes 10747904 | tf_op jit(solution)/shard_map/trp,scup->cstru/dot_general | solution.py:69
  53.7 17.6 %copy.33 = f32[16,4,8,64,64]{4,3,2,1,0:T(8,128)} copy(f32[16,4,8,64,64]{3,4,2,0,1:T(8,128)} %convolution_bitcast_fusion) | data formatting | bytes 16777216 | tf_op jit(solution)/shard_map/trp,scup->cstru/transpose | solution.py:69
  71.3 14.7 %reshape.468 = f32[64,8,4096]{2,1,0:T(8,128)} reshape(f32[16,4,8,64,64]{4,3,2,1,0:T(8,128)} %copy.33) | data formatting | bytes 16777216 | tf_op jit(solution)/shard_map/reshape | solution.py:77
  86.2 0.8 copy-done.7
  87.0 0.7 fusion.15
  88.4 1.8 copy.31
  90.2 81.4 %reduce-scatter.2.cloned.1.call-done = f32[4,8,4096]{2,1,0:T(8,128)} async-done(((f32[64,8,4096]{2,1,0:T(8,128)}), f32[4,8,4096]{2,1,0:T(8,128)}) %reduce-scatter.2.cloned.1.call-update) | async-done | bytes 524304 | tf_op jit(solution)/shard_map/reduce_scatter | solution.py:76
  171.7 1.5 reshape.469
  173.1 2.9 fusion.13
  176.0 56.6 %all-reduce.5.cloned.1.call-done = f32[4,64,128]{2,1,0:T(8,128)} async-done(((f32[4,64,128]{2,1,0:T(8,128)}), f32[4,64,128]{2,1,0:T(8,128)}) %all-reduce.5.cloned.1.call-update) | async-done | bytes 131088 | tf_op jit(solution)/shard_map/psum | solution.py:12
  232.6 3.9 fusion.9
  237.0 26.3 %collective-permute-done = f32[8,4,128,128]{2,3,0,1:T(8,128)} collective-permute-done((f32[8,4,128,128]{2,3,0,1:T(8,128)S(1)}, f32[8,4,128,128]{2,3,0,1:T(8,128)}, u32[]{:S(2)}, u32[]{:S(2)}) %collective-permute-start) | collective-permute-done | bytes 2097184 | tf_op jit(solution)/shard_map/ppermute | solution.py:17
  263.4 1.9 broadcast_select_fusion.1
  265.3 45.3 %collective-permute-done.1 = f32[8,4,128,128]{2,3,0,1:T(8,128)S(1)} collective-permute-done((f32[8,4,128,128]{2,3,0,1:T(8,128)S(1)}, f32[8,4,128,128]{2,3,0,1:T(8,128)S(1)}, u32[]{:S(2)}, u32[]{:S(2)}) %collective-permute-start.1) | collective-permute-done | bytes 2097184 | tf_op jit(solution)/shard_map/ppermute | solution.py:17
  310.7 0.4 broadcast_select_fusion.2
  311.1 0.8 collective-permute-start.2
  311.9 45.3 %collective-permute-done.2 = f32[8,4,128,128]{2,3,0,1:T(8,128)S(1)} collective-permute-done((f32[8,4,128,128]{2,3,0,1:T(8,128)S(1)}, f32[8,4,128,128]{2,3,0,1:T(8,128)S(1)}, u32[]{:S(2)}, u32[]{:S(2)}) %collective-permute-start.2) | collective-permute-done | bytes 2097184 | tf_op jit(solution)/shard_map/ppermute | solution.py:17
  357.2 0.4 broadcast_select_fusion.3
  357.6 2.1 collective-permute-start.3
  359.7 47.1 %collective-permute-done.3 = f32[8,4,128,128]{2,3,0,1:T(8,128)S(1)} collective-permute-done((f32[8,4,128,128]{2,3,0,1:T(8,128)S(1)}, f32[8,4,128,128]{2,3,0,1:T(8,128)S(1)}, u32[]{:S(2)}, u32[]{:S(2)}) %collective-permute-start.3) | collective-permute-done | bytes 2097184 | tf_op jit(solution)/shard_map/ppermute | solution.py:17
  406.8 0.4 broadcast_select_fusion.4
  407.3 49.8 %collective-permute-done.4 = f32[8,4,128,128]{2,3,0,1:T(8,128)S(1)} collective-permute-done((f32[8,4,128,128]{2,3,0,1:T(8,128)S(1)}, f32[8,4,128,128]{2,3,0,1:T(8,128)S(1)}, u32[]{:S(2)}, u32[]{:S(2)}) %collective-permute-start.4) | collective-permute-done | bytes 2097184 | tf_op jit(solution)/shard_map/ppermute | solution.py:17
  457.1 0.4 broadcast_select_fusion.5
  457.6 65.4 %collective-permute-done.5 = f32[8,4,128,128]{2,3,0,1:T(8,128)S(1)} collective-permute-done((f32[8,4,128,128]{2,3,0,1:T(8,128)S(1)}, f32[8,4,128,128]{2,3,0,1:T(8,128)S(1)}, u32[]{:S(2)}, u32[]{:S(2)}) %collective-permute-start.5) | collective-permute-done | bytes 2097184 | tf_op jit(solution)/shard_map/ppermute | solution.py:17
  522.9 0.3 broadcast_select_fusion.6
  524.5 26.5 %collective-permute-done.6 = f32[8,4,128,128]{2,3,0,1:T(8,128)} collective-permute-done((f32[8,4,128,128]{2,3,0,1:T(8,128)S(1)}, f32[8,4,128,128]{2,3,0,1:T(8,128)}, u32[]{:S(2)}, u32[]{:S(2)}) %collective-permute-start.6) | collective-permute-done | bytes 2097184 | tf_op jit(solution)/shard_map/ppermute | solution.py:17
  551.0 3.2 broadcast_select_fusion.7
  554.2 2.0 copy.35
  556.3 1.9 fusion.21
  558.2 13.0 %bitcast_add_fusion = f32[16,8,128,128]{3,1,2,0:T(8,128)S(1)} fusion(f32[16,1,8,1,128,128]{5,4,3,2,1,0:T(8,128)} %param.9, f32[16,4,128,128]{3,0,2,1:T(8,128)S(1)} %fusion.21, s32[4]{0:T(128)S(1)} %and_select_fusion), kind=kOutput, calls=%fused_computation.3 | convolution fusion | flops 102760480 | bytes 20971536 | tf_op jit(solution)/shard_map/bs,asxy->abxy/dot_general | solution.py:126
  571.2 1.2 broadcast.768
  572.4 5.8 broadcast_select_fusion
  578.2 1.1 select_bitcast_fusion.2
  579.3 1.6 select_bitcast_fusion
  580.9 0.2 all-reduce.7.cloned.1.call-start
  581.1 104.7 %all-reduce.9.cloned.1.call-done = (f32[16,128,128]{2,1,0:T(8,128)}, f32[16,128,128]{2,1,0:T(8,128)}, f32[16,128,128]{2,1,0:T(8,128)}, f32[16,128,128]{2,1,0:T(8,128)}) async-done(((f32[16,128,128]{2,1,0:T(8,128)}, f32[16,128,128]{2,1,0:T(8,128)}, f32[16,128,128]{2,1,0:T(8,128)}, f32[16,128,128]{2,1,0:T(8,128)}), (f32[16,128,128]{2,1,0:T(8,128)}, f32[16,128,128]{2,1,0:T(8,128)}, f32[16,128,128]{2,1,0:T(8,128)}, ...) | async-done | bytes 4194320 | tf_op jit(solution)/shard_map/psum | solution.py:12
  685.8 1.5 constant_dynamic-update-slice_fusion.3
  687.8 0.9 copy-done.4
  688.8 1.9 copy-done.2
  690.8 1.6 fusion.7
  692.5 9.9 %fusion.10 = f32[16,128,512]{2,1,0:T(8,128)} fusion(f32[16,128,512]{2,1,0:T(8,128)} %copy-done.2, f32[512,512]{1,0:T(8,128)S(1)} %copy-done), kind=kOutput, calls=%fused_computation.14 | convolution fusion | flops 6442450944 | bytes 9437184 | tf_op jit(solution)/shard_map/axp,pq->axq/dot_general | solution.py:138
  702.4 55.5 %all-reduce.7.cloned.1.call-done = f32[8,128,512]{2,1,0:T(8,128)} async-done(((f32[8,128,512]{2,1,0:T(8,128)}), f32[8,128,512]{2,1,0:T(8,128)}) %all-reduce.7.cloned.1.call-update) | async-done | bytes 2097168 | tf_op jit(solution)/shard_map/psum | solution.py:12
  757.9 18.0 %fusion.1 = f32[8,128,16,128]{3,1,2,0:T(8,128)} fusion(f32[16,128,512]{2,1,0:T(8,128)} %fusion.10, f32[8,128,512]{2,1,0:T(8,128)} %all-reduce.7.cloned.1.call-done), kind=kOutput, calls=%fused_computation.4 | convolution fusion | flops 12884901888 | bytes 14680064 | tf_op jit(solution)/shard_map/axq,byq->abxy/dot_general | solution.py:145
  775.9 9.4 %copy.42 = f32[8,128,16,128]{1,0,3,2:T(8,128)} copy(f32[8,128,16,128]{3,1,2,0:T(8,128)} %fusion.1) | data formatting | bytes 16777216 | tf_op jit(solution)/shard_map/axq,byq->abxy/dot_general | solution.py:145
  785.3 10.2 %fusion = f32[16,1,8,1,128,128]{5,2,4,0,3,1:T(8,128)} fusion(f32[16,8,128,128]{3,1,2,0:T(8,128)} %copy-done.1, f32[8,128,16,128]{1,0,3,2:T(8,128)} %copy.42, pred[16,8]{1,0:T(8,128)(4,1)S(1)} %compare_and_fusion), kind=kLoop, calls=%fused_computation.2 | loop fusion | flops 4194304 | bytes 25165952 | tf_op jit(solution)/shard_map/broadcast_in_dim | solution.py:152
  795.4 8.2 %copy.43 = f32[16,1,8,1,128,128]{5,4,3,2,1,0:T(8,128)} copy(f32[16,1,8,1,128,128]{5,2,4,0,3,1:T(8,128)} %fusion) | data formatting | bytes 16777216 | tf_op jit(solution)/shard_map/broadcast_in_dim | solution.py:152
  (56 shorter events, 2.6 us)
Async XLA Ops:
  6.5 686.0 %copy-start = (f32[512,512]{1,0:T(8,128)S(1)}, f32[512,512]{1,0:T(8,128)}, u32[]{:S(2)}) copy-start(f32[512,512]{1,0:T(8,128)} %param.15) | copy-start | bytes 3145732
  6.5 30.2 %all-gather.2.cloned.1.call-start = ((), (), s32[]{:S(2)}) async-start(), calls=%async_computation.2 | async-start | bytes 2359296 | tf_op jit(solution)/shard_map/all_gather | solution.py:66
  7.3 164.4 %reduce-scatter.2.cloned.1.call-start = ((), (), s32[]{:S(2)}) async-start(), calls=%async_computation.3 | async-start | bytes 8912896 | tf_op jit(solution)/shard_map/reduce_scatter | solution.py:76
  86.1 0.9 copy-start.7
  86.1 1.8 copy-start.8
  86.1 2.3 copy-start.3
  86.1 146.5 %all-reduce.5.cloned.1.call-start = ((), (), s32[]{:S(2)}) async-start(), calls=%async_computation.1 | async-start | bytes 262144 | tf_op jit(solution)/shard_map/psum | solution.py:12
  87.7 598.1 %all-reduce.9.cloned.1.call-start = ((), (), s32[]{:S(2)}) async-start(), calls=%async_computation.5 | async-start | bytes 8388608 | tf_op jit(solution)/shard_map/psum | solution.py:12
  176.0 60.6 %copy-start.9 = (s32[64]{0:T(128)S(1)}, s32[64]{0:T(128)}, u32[]{:S(2)}) copy-start(s32[64]{0:T(128)} %param.13) | copy-start | bytes 772
  236.6 26.8 %collective-permute-start = (f32[8,4,128,128]{2,3,0,1:T(8,128)S(1)}, f32[8,4,128,128]{2,3,0,1:T(8,128)}, u32[]{:S(2)}, u32[]{:S(2)}) collective-permute-start(f32[8,4,128,128]{2,3,0,1:T(8,128)S(1)} %fusion.9), channel_id=1, source_target_pairs={{0,16},{16,32},{32,48},{48,64},{64,80},{80,96},{96,112},{112,0},{1... | collective-permute-start | bytes 6291464 | tf_op jit(solution)/shard_map/ppermute | solution.py:17
  265.3 45.4 %collective-permute-start.1 = (f32[8,4,128,128]{2,3,0,1:T(8,128)S(1)}, f32[8,4,128,128]{2,3,0,1:T(8,128)S(1)}, u32[]{:S(2)}, u32[]{:S(2)}) collective-permute-start(f32[8,4,128,128]{2,3,0,1:T(8,128)S(1)} %broadcast_select_fusion.1), channel_id=1, source_target_pairs={{0,32},{16,48},{32,64},{48,80},{64,96},{80,112},{96,0},{112,16},{1... | collective-permute-start | bytes 6291464 | tf_op jit(solution)/shard_map/ppermute | solution.py:17
  311.1 46.1 %collective-permute-start.2 = (f32[8,4,128,128]{2,3,0,1:T(8,128)S(1)}, f32[8,4,128,128]{2,3,0,1:T(8,128)S(1)}, u32[]{:S(2)}, u32[]{:S(2)}) collective-permute-start(f32[8,4,128,128]{2,3,0,1:T(8,128)S(1)} %broadcast_select_fusion.2), channel_id=1, source_target_pairs={{0,64},{16,80},{32,96},{48,112},{64,0},{80,16},{96,32},{112,48},{1... | collective-permute-start | bytes 6291464 | tf_op jit(solution)/shard_map/ppermute | solution.py:17
  357.6 49.2 %collective-permute-start.3 = (f32[8,4,128,128]{2,3,0,1:T(8,128)S(1)}, f32[8,4,128,128]{2,3,0,1:T(8,128)S(1)}, u32[]{:S(2)}, u32[]{:S(2)}) collective-permute-start(f32[8,4,128,128]{2,3,0,1:T(8,128)S(1)} %broadcast_select_fusion.3), channel_id=1, source_target_pairs={{0,1},{1,2},{2,3},{3,4},{4,5},{5,6},{6,7},{7,8},{8,9},{9,10},{10,1... | collective-permute-start | bytes 6291464 | tf_op jit(solution)/shard_map/ppermute | solution.py:17
  407.2 49.9 %collective-permute-start.4 = (f32[8,4,128,128]{2,3,0,1:T(8,128)S(1)}, f32[8,4,128,128]{2,3,0,1:T(8,128)S(1)}, u32[]{:S(2)}, u32[]{:S(2)}) collective-permute-start(f32[8,4,128,128]{2,3,0,1:T(8,128)S(1)} %broadcast_select_fusion.4), channel_id=1, source_target_pairs={{0,2},{1,3},{2,4},{3,5},{4,6},{5,7},{6,8},{7,9},{8,10},{9,11},{10,... | collective-permute-start | bytes 6291464 | tf_op jit(solution)/shard_map/ppermute | solution.py:17
  457.5 65.5 %collective-permute-start.5 = (f32[8,4,128,128]{2,3,0,1:T(8,128)S(1)}, f32[8,4,128,128]{2,3,0,1:T(8,128)S(1)}, u32[]{:S(2)}, u32[]{:S(2)}) collective-permute-start(f32[8,4,128,128]{2,3,0,1:T(8,128)S(1)} %broadcast_select_fusion.5), channel_id=1, source_target_pairs={{0,4},{1,5},{2,6},{3,7},{4,8},{5,9},{6,10},{7,11},{8,12},{9,13},{1... | collective-permute-start | bytes 6291464 | tf_op jit(solution)/shard_map/ppermute | solution.py:17
  523.3 27.7 %collective-permute-start.6 = (f32[8,4,128,128]{2,3,0,1:T(8,128)S(1)}, f32[8,4,128,128]{2,3,0,1:T(8,128)}, u32[]{:S(2)}, u32[]{:S(2)}) collective-permute-start(f32[8,4,128,128]{2,3,0,1:T(8,128)S(1)} %broadcast_select_fusion.6), channel_id=1, source_target_pairs={{0,8},{1,9},{2,10},{3,11},{4,12},{5,13},{6,14},{7,15},{8,0},{9,1},... | collective-permute-start | bytes 6291464 | tf_op jit(solution)/shard_map/ppermute | solution.py:17
  571.2 7.0 copy-start.1
  580.9 177.0 %all-reduce.7.cloned.1.call-start = ((), (), s32[]{:S(2)}) async-start(), calls=%async_computation.4 | async-start | bytes 4194304 | tf_op jit(solution)/shard_map/psum | solution.py:12
  685.8 1.5 copy-start.6
  685.8 1.9 copy-start.5
  687.4 1.3 copy-start.4
  688.8 2.0 copy-start.2
Sparse Core Ops, SparseCore 0:
  9.1 27.6 all-gather.1
  86.2 85.3 reduce-scatter.1
  174.0 58.6 all-reduce.4
  581.0 104.7 all-reduce.8
  692.5 65.3 all-reduce.6
where the time goes:
time: 820 us; the launch traced here: 810 us
  waiting for transfers between devices  634 us (77%)
  matrix products  66.6 us (8%)
  local copies, waits for them, and re-layouts  62.5 us (8%)
  other arithmetic  29.3 us (4%)
  between operations  14.4 us (2%)
    ppermute x7, waiting for transfers between devices, from_behind(): return lax.ppermute(x, axis, [(i, (i + by) % count) for i in range(count)])  306 us
    psum x3, waiting for transfers between devices, spread_2(): return lax.psum(jnp.where(mine, x, jnp.zeros_like(x)), axis)  217 us
    reduce_scatter x1, waiting for transfers between devices, per_device(): lax.psum_scatter(products.reshape(lax.axis_size('col') * local_cols, loca...  81.4 us
    all_gather x1, waiting for transfers between devices, per_device(): all_pivots = lax.all_gather(pivot_basis, 'row', axis=1, tiled=True)  29.4 us
    dot_general x1, matrix products, per_device(): jnp.einsum('axq,byq->abxy', scaled, col_panel, precision=highest, preferr...  18 us
    transpose x1, local copies, waits for them, and re-layouts, per_device(): jnp.einsum('trp,scup->cstru', own_pivots, grouped, precision=highest, pre...  17.6 us
    dot_general x1, matrix products, per_device(): jnp.einsum('trp,scup->cstru', own_pivots, grouped, precision=highest, pre...  17 us
  transfers between devices with their start and end apart: 12, of which 12 were waited for; matrix products, arithmetic and copies ran while one was open for 2% of the time, Pallas kernels for 0%

commit v1 on v0

--- a/solution.py
+++ b/solution.py
@@ -9,7 +9,12 @@
 
 def spread_2(x, axis, root):
     mine = lax.axis_index(axis) == root
-    return lax.psum(jnp.where(mine, x, jnp.zeros_like(x)), axis)
+
+    def load_arrays_by_axis(load):
+        t1 = lax.all_gather(load, axis_name=axis).sum(axis=0)
+        return t1
+
+    return load_arrays_by_axis(jnp.where(mine, x, jnp.zeros_like(x)))
 
 
 def from_behind(x, axis, by):

time: 820 us -> 1130 us (1.38)
  waiting for transfers between devices: 634 us -> 910 us
  other arithmetic: 29.3 us -> 70.6 us
    all_gather x0 -> x6, waiting for transfers between devices: none -> 500 us  [load_arrays_by_axis(): t1 = lax.all_gather(load, axis_name=axis).sum(axis=0)]
    psum x3 -> x0, waiting for transfers between devices: 217 us -> none  [spread_2(): return lax.psum(jnp.where(mine, x, jnp.zeros_like(x)), axis)]
    reduce_sum x0 -> x6, other arithmetic: none -> 41.1 us  [load_arrays_by_axis(): t1 = lax.all_gather(load, axis_name=axis).sum(axis=0)]
  transfers between devices with their start and end apart: 12 -> 15, of which waited for: 12 -> 14; matrix products, arithmetic and copies ran while one was open for 2% -> 8% of each run, Pallas kernels for 0% -> 0%
where the time goes in v1:
time: 1130 us; the launch traced here: 1120 us
  waiting for transfers between devices  910 us (81%)
  other arithmetic  70.6 us (6%)
  matrix products  64.4 us (6%)
  local copies, waits for them, and re-layouts  57 us (5%)
  between operations  15 us (1%)
    all_gather x6, waiting for transfers between devices, load_arrays_by_axis(): t1 = lax.all_gather(load, axis_name=axis).sum(axis=0)  500 us
    ppermute x7, waiting for transfers between devices, from_behind(): return lax.ppermute(x, axis, [(i, (i + by) % count) for i in range(count)])  299 us
    reduce_scatter x1, waiting for transfers between devices, per_device(): lax.psum_scatter(products.reshape(lax.axis_size('col') * local_cols, loca...  80.3 us
    reduce_sum x6, other arithmetic, load_arrays_by_axis(): t1 = lax.all_gather(load, axis_name=axis).sum(axis=0)  41.1 us
    all_gather x1, waiting for transfers between devices, per_device(): all_pivots = lax.all_gather(pivot_basis, 'row', axis=1, tiled=True)  27.7 us
  transfers between devices with their start and end apart: 15, of which 14 were waited for; matrix products, arithmetic and copies ran while one was open for 8% of the time, Pallas kernels for 0%

profile of v1, /device:TPU:0, one launch (start us, length us, event | category | flops | bytes accessed | tf_op | source)
XLA Modules:
  0.0 1121.2 jit_solution(16645495647349369451)
XLA Ops:
  6.5 0.7 all-gather.14.cloned.1.call-update
  7.3 1.6 dynamic-slice_select_fusion.1
  9.0 27.7 %all-gather.14.cloned.1.call-done = f32[8,8,64,128]{3,2,1,0:T(8,128)} async-done(((f32[8,1,64,128]{3,2,1,0:T(8,128)}), f32[8,8,64,128]{3,2,1,0:T(8,128)}) %all-gather.14.cloned.1.call-update) | async-done | bytes 2097168 | tf_op jit(solution)/shard_map/all_gather | solution.py:71
  36.7 16.9 %convolution_bitcast_fusion = f32[16,4,8,64,64]{3,4,2,0,1:T(8,128)} fusion(f32[4,16,64,128,1]{3,2,4,1,0:T(8,128)} %bitcast.111, f32[8,1,64,128]{3,2,1,0:T(8,128)} %param.11), kind=kOutput, calls=%fused_computation.6 | convolution fusion | flops 3221225472 | bytes 10747904 | tf_op jit(solution)/shard_map/trp,scup->cstru/dot_general | solution.py:74
  53.7 17.7 %copy.32 = f32[16,4,8,64,64]{4,3,2,1,0:T(8,128)} copy(f32[16,4,8,64,64]{3,4,2,0,1:T(8,128)} %convolution_bitcast_fusion) | data formatting | bytes 16777216 | tf_op jit(solution)/shard_map/trp,scup->cstru/transpose | solution.py:74
  71.4 14.7 %reshape.528 = f32[64,8,4096]{2,1,0:T(8,128)} reshape(f32[16,4,8,64,64]{4,3,2,1,0:T(8,128)} %copy.32) | data formatting | bytes 16777216 | tf_op jit(solution)/shard_map/reshape | solution.py:82
  86.2 1.5 copy-done.2
  87.7 1.9 copy.31
  90.2 1.3 bitcast_reduce_fusion.5
  91.5 80.3 %reduce-scatter.2.cloned.1.call-done = f32[4,8,4096]{2,1,0:T(8,128)} async-done(((f32[64,8,4096]{2,1,0:T(8,128)}), f32[4,8,4096]{2,1,0:T(8,128)}) %reduce-scatter.2.cloned.1.call-update) | async-done | bytes 524304 | tf_op jit(solution)/shard_map/reduce_scatter | solution.py:81
  171.8 1.5 reshape.529
  173.3 1.9 fusion.12
  175.2 3.6 fusion.8
  179.2 26.3 %collective-permute-done = f32[8,4,128,128]{2,3,0,1:T(8,128)} collective-permute-done((f32[8,4,128,128]{2,3,0,1:T(8,128)S(1)}, f32[8,4,128,128]{2,3,0,1:T(8,128)}, u32[]{:S(2)}, u32[]{:S(2)}) %collective-permute-start) | collective-permute-done | bytes 2097184 | tf_op jit(solution)/shard_map/ppermute | solution.py:22
  205.6 1.9 broadcast_select_fusion.4
  207.8 46.3 %collective-permute-done.1 = f32[8,4,128,128]{2,3,0,1:T(8,128)S(1)} collective-permute-done((f32[8,4,128,128]{2,3,0,1:T(8,128)S(1)}, f32[8,4,128,128]{2,3,0,1:T(8,128)S(1)}, u32[]{:S(2)}, u32[]{:S(2)}) %collective-permute-start.1) | collective-permute-done | bytes 2097184 | tf_op jit(solution)/shard_map/ppermute | solution.py:22
  254.5 1.6 collective-permute-start.2
  256.1 44.4 %collective-permute-done.2 = f32[8,4,128,128]{2,3,0,1:T(8,128)S(1)} collective-permute-done((f32[8,4,128,128]{2,3,0,1:T(8,128)S(1)}, f32[8,4,128,128]{2,3,0,1:T(8,128)S(1)}, u32[]{:S(2)}, u32[]{:S(2)}) %collective-permute-start.2) | collective-permute-done | bytes 2097184 | tf_op jit(solution)/shard_map/ppermute | solution.py:22
  300.9 1.5 collective-permute-start.3
  302.5 46.8 %collective-permute-done.3 = f32[8,4,128,128]{2,3,0,1:T(8,128)S(1)} collective-permute-done((f32[8,4,128,128]{2,3,0,1:T(8,128)S(1)}, f32[8,4,128,128]{2,3,0,1:T(8,128)S(1)}, u32[]{:S(2)}, u32[]{:S(2)}) %collective-permute-start.3) | collective-permute-done | bytes 2097184 | tf_op jit(solution)/shard_map/ppermute | solution.py:22
  349.8 49.8 %collective-permute-done.4 = f32[8,4,128,128]{2,3,0,1:T(8,128)S(1)} collective-permute-done((f32[8,4,128,128]{2,3,0,1:T(8,128)S(1)}, f32[8,4,128,128]{2,3,0,1:T(8,128)S(1)}, u32[]{:S(2)}, u32[]{:S(2)}) %collective-permute-start.4) | collective-permute-done | bytes 2097184 | tf_op jit(solution)/shard_map/ppermute | solution.py:22
  400.1 59.1 %collective-permute-done.5 = f32[8,4,128,128]{2,3,0,1:T(8,128)S(1)} collective-permute-done((f32[8,4,128,128]{2,3,0,1:T(8,128)S(1)}, f32[8,4,128,128]{2,3,0,1:T(8,128)S(1)}, u32[]{:S(2)}, u32[]{:S(2)}) %collective-permute-start.5) | collective-permute-done | bytes 2097184 | tf_op jit(solution)/shard_map/ppermute | solution.py:22
  460.8 26.5 %collective-permute-done.6 = f32[8,4,128,128]{2,3,0,1:T(8,128)} collective-permute-done((f32[8,4,128,128]{2,3,0,1:T(8,128)S(1)}, f32[8,4,128,128]{2,3,0,1:T(8,128)}, u32[]{:S(2)}, u32[]{:S(2)}) %collective-permute-start.6) | collective-permute-done | bytes 2097184 | tf_op jit(solution)/shard_map/ppermute | solution.py:22
  487.3 3.2 broadcast_select_fusion.10
  490.5 2.0 copy.34
  492.5 1.9 fusion.19
  494.4 13.0 %bitcast_add_fusion = f32[16,8,128,128]{3,1,2,0:T(8,128)S(1)} fusion(f32[16,1,8,1,128,128]{5,4,3,2,1,0:T(8,128)} %param.9, f32[16,4,128,128]{3,0,2,1:T(8,128)S(1)} %fusion.19, s32[4]{0:T(128)S(1)} %and_select_fusion), kind=kOutput, calls=%fused_computation.8 | convolution fusion | flops 102760480 | bytes 20971536 | tf_op jit(solution)/shard_map/bs,asxy->abxy/dot_general | solution.py:131
  507.5 5.9 broadcast_select_fusion.3
  513.4 0.5 all-gather.22.cloned.1.call-update
  514.0 0.5 all-gather.20.cloned.1.call-update
  514.6 0.7 all-gather.18.cloned.1.call-update
  515.5 109.0 %all-gather.24.cloned.1.call-done = f32[256,1,128,128]{3,2,1,0:T(8,128)} async-done(((f32[16,1,128,128]{3,2,1,0:T(8,128)}), f32[256,1,128,128]{3,2,1,0:T(8,128)}) %all-gather.24.cloned.1.call-update) | async-done | bytes 16777232 | tf_op jit(solution)/shard_map/all_gather | solution.py:14
  624.5 7.4 bitcast_reduce_fusion.1
  632.0 105.6 %all-gather.22.cloned.1.call-done = f32[256,1,128,128]{3,2,1,0:T(8,128)} async-done(((f32[16,1,128,128]{3,2,1,0:T(8,128)}), f32[256,1,128,128]{3,2,1,0:T(8,128)}) %all-gather.22.cloned.1.call-update) | async-done | bytes 16777232 | tf_op jit(solution)/shard_map/all_gather | solution.py:14
  737.6 7.4 bitcast_reduce_fusion.2
  745.1 105.6 %all-gather.20.cloned.1.call-done = f32[256,1,128,128]{3,2,1,0:T(8,128)} async-done(((f32[16,1,128,128]{3,2,1,0:T(8,128)}), f32[256,1,128,128]{3,2,1,0:T(8,128)}) %all-gather.20.cloned.1.call-update) | async-done | bytes 16777232 | tf_op jit(solution)/shard_map/all_gather | solution.py:14
  850.7 8.4 bitcast_reduce_fusion.3
  859.1 104.8 %all-gather.18.cloned.1.call-done = f32[256,1,128,128]{3,2,1,0:T(8,128)} async-done(((f32[16,1,128,128]{3,2,1,0:T(8,128)}), f32[256,1,128,128]{3,2,1,0:T(8,128)}) %all-gather.18.cloned.1.call-update) | async-done | bytes 16777232 | tf_op jit(solution)/shard_map/all_gather | solution.py:14
  963.9 8.4 bitcast_reduce_fusion.4
  972.3 1.8 pad_maximum_fusion
  974.2 1.7 dynamic-slice_select_fusion
  976.0 9.5 fusion.9
  985.5 75.1 %all-gather.26.cloned.1.call-done = f32[64,1,128,512]{3,2,1,0:T(8,128)} async-done(((f32[8,1,128,512]{3,2,1,0:T(8,128)}), f32[64,1,128,512]{3,2,1,0:T(8,128)}) %all-gather.26.cloned.1.call-update) | async-done | bytes 16777232 | tf_op jit(solution)/shard_map/all_gather | solution.py:14
  1060.6 8.1 bitcast_reduce_fusion
  1068.7 17.6 %fusion.1 = f32[8,128,16,128]{3,1,2,0:T(8,128)} fusion(f32[16,128,512]{2,1,0:T(8,128)} %fusion.9, f32[8,128,512]{2,1,0:T(8,128)S(1)} %bitcast_reduce_fusion), kind=kOutput, calls=%fused_computation.10 | convolution fusion | flops 12884901888 | bytes 14680064 | tf_op jit(solution)/shard_map/axq,byq->abxy/dot_general | solution.py:150
  1086.3 9.3 copy.40
  1095.5 10.1 fusion
  1105.7 8.2 copy.41
  (57 shorter events, 4.6 us)
Async XLA Ops:
  6.5 969.5 %copy-start = (f32[512,512]{1,0:T(8,128)S(1)}, f32[512,512]{1,0:T(8,128)}, u32[]{:S(2)}) copy-start(f32[512,512]{1,0:T(8,128)} %param.15) | copy-start | bytes 3145732
  6.5 30.2 %all-gather.14.cloned.1.call-start = ((), (), s32[]{:S(2)}) async-start(), calls=%async_computation.1 | async-start | bytes 2359296 | tf_op jit(solution)/shard_map/all_gather | solution.py:71
  7.3 82.9 %all-gather.16.cloned.1.call-start = ((), (), s32[]{:S(2)}) async-start(), calls=%async_computation.3 | async-start | bytes 1179648 | tf_op jit(solution)/shard_map/all_gather | solution.py:14
  8.9 162.9 %reduce-scatter.2.cloned.1.call-start = ((), (), s32[]{:S(2)}) async-start(), calls=%async_computation.2 | async-start | bytes 8912896 | tf_op jit(solution)/shard_map/reduce_scatter | solution.py:81
  86.1 1.6 copy-start.2
  86.1 3.5 copy-start.4
  86.1 538.4 %all-gather.24.cloned.1.call-start = ((), (), s32[]{:S(2)}) async-start(), calls=%async_computation.7 | async-start | bytes 17825792 | tf_op jit(solution)/shard_map/all_gather | solution.py:14
  89.6 83.7 %copy-start.3 = (f32[8,1,64,128]{3,2,1,0:T(8,128)S(1)}, f32[8,1,64,128]{3,2,1,0:T(8,128)}, u32[]{:S(2)}) copy-start(f32[8,1,64,128]{3,2,1,0:T(8,128)} %param.10) | copy-start | bytes 786436
  175.2 3.6 copy-start.5
  178.8 26.8 %collective-permute-start = (f32[8,4,128,128]{2,3,0,1:T(8,128)S(1)}, f32[8,4,128,128]{2,3,0,1:T(8,128)}, u32[]{:S(2)}, u32[]{:S(2)}) collective-permute-start(f32[8,4,128,128]{2,3,0,1:T(8,128)S(1)} %fusion.8), channel_id=1, source_target_pairs={{0,16},{16,32},{32,48},{48,64},{64,80},{80,96},{96,112},{112,0},{1... | collective-permute-start | bytes 6291464 | tf_op jit(solution)/shard_map/ppermute | solution.py:22
  207.5 46.6 %collective-permute-start.1 = (f32[8,4,128,128]{2,3,0,1:T(8,128)S(1)}, f32[8,4,128,128]{2,3,0,1:T(8,128)S(1)}, u32[]{:S(2)}, u32[]{:S(2)}) collective-permute-start(f32[8,4,128,128]{2,3,0,1:T(8,128)S(1)} %broadcast_select_fusion.4), channel_id=1, source_target_pairs={{0,32},{16,48},{32,64},{48,80},{64,96},{80,112},{96,0},{112,16},{1... | collective-permute-start | bytes 6291464 | tf_op jit(solution)/shard_map/ppermute | solution.py:22
  254.5 46.0 %collective-permute-start.2 = (f32[8,4,128,128]{2,3,0,1:T(8,128)S(1)}, f32[8,4,128,128]{2,3,0,1:T(8,128)S(1)}, u32[]{:S(2)}, u32[]{:S(2)}) collective-permute-start(f32[8,4,128,128]{2,3,0,1:T(8,128)S(1)} %broadcast_select_fusion.5), channel_id=1, source_target_pairs={{0,64},{16,80},{32,96},{48,112},{64,0},{80,16},{96,32},{112,48},{1... | collective-permute-start | bytes 6291464 | tf_op jit(solution)/shard_map/ppermute | solution.py:22
  300.9 48.4 %collective-permute-start.3 = (f32[8,4,128,128]{2,3,0,1:T(8,128)S(1)}, f32[8,4,128,128]{2,3,0,1:T(8,128)S(1)}, u32[]{:S(2)}, u32[]{:S(2)}) collective-permute-start(f32[8,4,128,128]{2,3,0,1:T(8,128)S(1)} %broadcast_select_fusion.6), channel_id=1, source_target_pairs={{0,1},{1,2},{2,3},{3,4},{4,5},{5,6},{6,7},{7,8},{8,9},{9,10},{10,1... | collective-permute-start | bytes 6291464 | tf_op jit(solution)/shard_map/ppermute | solution.py:22
  349.7 49.9 %collective-permute-start.4 = (f32[8,4,128,128]{2,3,0,1:T(8,128)S(1)}, f32[8,4,128,128]{2,3,0,1:T(8,128)S(1)}, u32[]{:S(2)}, u32[]{:S(2)}) collective-permute-start(f32[8,4,128,128]{2,3,0,1:T(8,128)S(1)} %broadcast_select_fusion.7), channel_id=1, source_target_pairs={{0,2},{1,3},{2,4},{3,5},{4,6},{5,7},{6,8},{7,9},{8,10},{9,11},{10,... | collective-permute-start | bytes 6291464 | tf_op jit(solution)/shard_map/ppermute | solution.py:22
  400.0 59.2 %collective-permute-start.5 = (f32[8,4,128,128]{2,3,0,1:T(8,128)S(1)}, f32[8,4,128,128]{2,3,0,1:T(8,128)S(1)}, u32[]{:S(2)}, u32[]{:S(2)}) collective-permute-start(f32[8,4,128,128]{2,3,0,1:T(8,128)S(1)} %broadcast_select_fusion.8), channel_id=1, source_target_pairs={{0,4},{1,5},{2,6},{3,7},{4,8},{5,9},{6,10},{7,11},{8,12},{9,13},{1... | collective-permute-start | bytes 6291464 | tf_op jit(solution)/shard_map/ppermute | solution.py:22
  459.5 27.7 %collective-permute-start.6 = (f32[8,4,128,128]{2,3,0,1:T(8,128)S(1)}, f32[8,4,128,128]{2,3,0,1:T(8,128)}, u32[]{:S(2)}, u32[]{:S(2)}) collective-permute-start(f32[8,4,128,128]{2,3,0,1:T(8,128)S(1)} %broadcast_select_fusion.9), channel_id=1, source_target_pairs={{0,8},{1,9},{2,10},{3,11},{4,12},{5,13},{6,14},{7,15},{8,0},{9,1},... | collective-permute-start | bytes 6291464 | tf_op jit(solution)/shard_map/ppermute | solution.py:22
  507.4 5.9 copy-start.1
  513.4 224.3 %all-gather.22.cloned.1.call-start = ((), (), s32[]{:S(2)}) async-start(), calls=%async_computation.6 | async-start | bytes 17825792 | tf_op jit(solution)/shard_map/all_gather | solution.py:14
  514.0 336.7 %all-gather.20.cloned.1.call-start = ((), (), s32[]{:S(2)}) async-start(), calls=%async_computation.5 | async-start | bytes 17825792 | tf_op jit(solution)/shard_map/all_gather | solution.py:14
  514.5 449.4 %all-gather.18.cloned.1.call-start = ((), (), s32[]{:S(2)}) async-start(), calls=%async_computation.4 | async-start | bytes 17825792 | tf_op jit(solution)/shard_map/all_gather | solution.py:14
  515.3 545.3 %all-gather.26.cloned.1.call-start = ((), (), s32[]{:S(2)}) async-start(), calls=%async_computation.8 | async-start | bytes 18874368 | tf_op jit(solution)/shard_map/all_gather | solution.py:14
Sparse Core Ops, SparseCore 0:
  9.1 27.6 all-gather.13
  38.4 23.6 all-gather.15
  86.2 85.5 reduce-scatter.1
  513.5 111.0 all-gather.23
  626.5 111.0 all-gather.21
  739.6 111.0 all-gather.19
  852.8 111.0 all-gather.17
  976.0 84.5 all-gather.25
